TPU v7x, 32 devices: a whole 2x2x4 slice. The times are simulated.
32 devices in a mesh: seq: 4 (over y, x), head: 4 (over z), rep: 2 (over core).
Axes of the slice: x: 2, y: 2, z: 4, core: 2. Of those that a mesh axis runs over, the one named last changes fastest.
Arguments:
- query_heads: bfloat16 [2, 8192, 4096], P('rep', 'seq', 'head'), may hold values from -0.59765625 to 0.59765625
- key_heads: bfloat16 [2, 8192, 4096], P('rep', 'seq', 'head'), may hold values from -0.59765625 to 0.59765625
- value_heads: bfloat16 [2, 8192, 4096], P('rep', 'seq', 'head'), may hold values from -6 to 6
- out_cotangent: bfloat16 [2, 8192, 4096], P('rep', 'seq', 'head'), may hold values from -0.19921875 to 0.19921875
- out_weight: bfloat16 [4096, 4096], P('head'), may hold values from -0.09375 to 0.09375
- doc_ends: int32 [2, 7], P('rep'), may hold values from 1 to 8192, as said below
Outputs:
- grad_query: bfloat16 [2, 8192, 4096], P('rep', 'seq', 'head')
- grad_key: bfloat16 [2, 8192, 4096], P('rep', 'seq', 'head')
- grad_value: bfloat16 [2, 8192, 4096], P('rep', 'seq', 'head')
- grad_weight: float32 [4096, 4096], P('head', ('seq', 'rep'))
Inputs may be any that keep to these rules, and one draw needn't show every extreme that they name: `doc_ends`: each row holds 7 strictly increasing document end offsets; its last entry is 8192.
All inputs are finite; a program needn't handle non-finite values.
Results may differ from a plain program's by a relative error of at most 0.0052.
Values may be sent and summed in bfloat16 or wider, within the bound.
No kernel may reach another device: no remote copies, remote signals or barrier semaphores. Data moves between devices by JAX's collectives and lax.ppermute only.
A program may use at most 320 MiB of HBM per device.

v0:
```python
import jax
import jax.numpy as jnp
from jax import lax
from jax.sharding import PartitionSpec as P

HD = 128
BLOCK = 512
highest = lax.Precision.HIGHEST


def prefix(shard, axis, combine, identity, reverse):
    count, here = (lax.axis_size(axis), lax.axis_index(axis))
    everything = jax.tree.map(lambda part: lax.all_gather(part, axis), shard)
    start = jax.tree.map(
        lambda part, zero: jnp.broadcast_to(jnp.asarray(zero, part.dtype), part.shape),
        shard,
        identity,
    )

    def step(k, before):
        at = count - 1 - k if reverse else k
        reached = at > here if reverse else at < here
        new = combine(before, jax.tree.map(lambda part: part[at], everything))
        return jax.tree.map(lambda a, b: jnp.where(reached, a, b), new, before)

    return lax.fori_loop(0, count, step, start)


def doc_counts(positions, ends_row):
    return jnp.sum((ends_row[None, :] <= positions[:, None]).astype(jnp.int32), axis=1)


def local_pass(queries, keys, values, grads, counts, count_before):
    length, heads, width = queries.shape
    blocks = length // BLOCK
    query_blocks = queries.reshape(blocks, BLOCK, heads, width)
    key_blocks = keys.reshape(blocks, BLOCK, heads, width)
    value_blocks = values.reshape(blocks, BLOCK, heads, width)
    grad_blocks = grads.reshape(blocks, BLOCK, heads, width)
    count_blocks = counts.reshape(blocks, BLOCK)
    before_each = jnp.concatenate([jnp.reshape(count_before, (1,)), count_blocks[:-1, -1]])
    last_each = count_blocks[:, -1]
    rows = lax.broadcasted_iota(jnp.int32, (BLOCK, BLOCK), 0)
    cols = lax.broadcasted_iota(jnp.int32, (BLOCK, BLOCK), 1)
    allowed = (
        (count_blocks[:, :, None] == count_blocks[:, None, :]) & (rows >= cols)[None]
    ).astype(jnp.float32)
    scores = jnp.einsum(
        "nthe,nshe->nhts", query_blocks, key_blocks, preferred_element_type=jnp.float32
    )
    attn = (scores * allowed[:, None]).astype(jnp.bfloat16)
    back = jnp.einsum(
        "nthe,nshe->nhts", grad_blocks, value_blocks, preferred_element_type=jnp.float32
    )
    pgrad = (back * allowed[:, None]).astype(jnp.bfloat16)
    out_intra = jnp.einsum(
        "nhts,nshe->nthe", attn, value_blocks, preferred_element_type=jnp.float32
    )
    dq_intra = jnp.einsum("nhts,nshe->nthe", pgrad, key_blocks, preferred_element_type=jnp.float32)
    dk_intra = jnp.einsum(
        "nhts,nthe->nshe", pgrad, query_blocks, preferred_element_type=jnp.float32
    )
    dv_intra = jnp.einsum("nhts,nthe->nshe", attn, grad_blocks, preferred_element_type=jnp.float32)
    first_match = (count_blocks == before_each[:, None])[:, :, None, None]
    last_match = (count_blocks == last_each[:, None])[:, :, None, None]
    keep = (last_each == before_each).astype(jnp.float32)
    tails = jnp.einsum(
        "nshe,nshf->nhef",
        key_blocks * last_match.astype(jnp.bfloat16),
        value_blocks,
        preferred_element_type=jnp.float32,
    )
    head_sums = jnp.einsum(
        "nthe,nthf->nhef",
        query_blocks * first_match.astype(jnp.bfloat16),
        grad_blocks,
        preferred_element_type=jnp.float32,
    )

    def link_step(state, item):
        return (item[0] + item[1] * state, state)

    empty = jnp.zeros((heads, width, width), jnp.float32)
    final_tail, states_before = lax.scan(link_step, empty, (tails, keep))
    final_head, states_after = lax.scan(link_step, empty, (head_sums, keep), reverse=True)
    first_weight = first_match.astype(jnp.float32)
    last_weight = last_match.astype(jnp.float32)
    outputs = out_intra + first_weight * jnp.einsum(
        "nthe,nhef->nthf", query_blocks.astype(jnp.float32), states_before, precision=highest
    )
    dq = dq_intra + first_weight * jnp.einsum(
        "nthf,nhef->nthe", grad_blocks.astype(jnp.float32), states_before, precision=highest
    )
    dk = dk_intra + last_weight * jnp.einsum(
        "nshf,nhef->nshe", value_blocks.astype(jnp.float32), states_after, precision=highest
    )
    dv = dv_intra + last_weight * jnp.einsum(
        "nshe,nhef->nshf", key_blocks.astype(jnp.float32), states_after, precision=highest
    )
    shape = (length, heads, width)
    return (
        outputs.reshape(shape),
        dq.reshape(shape),
        dk.reshape(shape),
        dv.reshape(shape),
        final_tail,
        final_head,
    )


def link_states(earlier, later):
    return (jnp.maximum(earlier[0], later[0]), later[1] + (1.0 - later[0]) * earlier[1])


def on_device(query_heads, key_heads, value_heads, out_cotangent, out_weight, doc_ends):
    length = query_heads.shape[1]
    heads = query_heads.shape[2] // HD
    queries = query_heads[0].reshape(length, heads, HD)
    keys = key_heads[0].reshape(length, heads, HD)
    values = value_heads[0].reshape(length, heads, HD)
    full_cotangent = lax.all_gather(out_cotangent, "head", axis=2, tiled=True)[0]
    grads_flat = lax.dot_general(
        full_cotangent, out_weight, (((1,), (1,)), ((), ())), preferred_element_type=jnp.float32
    ).astype(jnp.bfloat16)
    grads = grads_flat.reshape(length, heads, HD)
    offset = lax.axis_index("seq") * length
    positions = offset + jnp.arange(length, dtype=jnp.int32)
    ends_row = doc_ends[0]
    counts = doc_counts(positions, ends_row)
    count_before = doc_counts(jnp.reshape(offset - 1, (1,)), ends_row)[0]
    outputs, dq, dk, dv, tail, head = local_pass(queries, keys, values, grads, counts, count_before)
    flag = (counts[-1] != count_before).astype(jnp.float32)
    identity = (jnp.zeros((), jnp.float32), jnp.zeros_like(tail))
    flag_before, carry_before = prefix((flag, tail), "seq", link_states, identity, False)
    flag_after, carry_after = prefix((flag, head), "seq", link_states, identity, True)
    entry_weight = (counts == count_before).astype(jnp.float32)[:, None, None]
    exit_weight = (counts == counts[-1]).astype(jnp.float32)[:, None, None]
    outputs = outputs + entry_weight * jnp.einsum(
        "the,hef->thf", queries.astype(jnp.float32), carry_before, precision=highest
    )
    dq = dq + entry_weight * jnp.einsum(
        "thf,hef->the", grads.astype(jnp.float32), carry_before, precision=highest
    )
    dk = dk + exit_weight * jnp.einsum(
        "thf,hef->the", values.astype(jnp.float32), carry_after, precision=highest
    )
    dv = dv + exit_weight * jnp.einsum(
        "the,hef->thf", keys.astype(jnp.float32), carry_after, precision=highest
    )
    flat = heads * HD
    attention_out = outputs.reshape(length, flat).astype(jnp.bfloat16)
    grad_query = dq.reshape(1, length, flat).astype(jnp.bfloat16)
    grad_key = dk.reshape(1, length, flat).astype(jnp.bfloat16)
    grad_value = dv.reshape(1, length, flat).astype(jnp.bfloat16)
    partial_grad = lax.dot_general(
        attention_out, full_cotangent, (((0,), (0,)), ((), ())), preferred_element_type=jnp.float32
    )
    summed = lax.psum(partial_grad, ("seq", "rep"))
    columns = summed.shape[1] // lax.axis_size(("seq", "rep"))
    grad_weight = lax.dynamic_slice_in_dim(
        summed, lax.axis_index(("seq", "rep")) * columns, columns, 1
    )
    return (grad_query, grad_key, grad_value, grad_weight)


def solution(mesh):
    in_specs = (
        P("rep", "seq", "head"),
        P("rep", "seq", "head"),
        P("rep", "seq", "head"),
        P("rep", "seq", "head"),
        P("head", None),
        P("rep", None),
    )
    out_specs = (
        P("rep", "seq", "head"),
        P("rep", "seq", "head"),
        P("rep", "seq", "head"),
        P("head", ("seq", "rep")),
    )
    return jax.shard_map(
        on_device, mesh=mesh, in_specs=in_specs, out_specs=out_specs, check_vma=False
    )
```

profile of v0, /device:TPU:0, one launch (start us, length us, event | category | flops | bytes accessed | tf_op | source)
XLA Modules:
  0.0 711.5 jit_solution(5314023280602779764)
XLA Ops:
  8.4 5.4 copy.224
  13.8 3.1 copy.225
  16.9 7.6 %copy.175 = bf16[4,512,8,128]{1,3,2,0:T(8,128)(2,1)} copy(bf16[4,512,8,128]{3,2,1,0:T(8,128)(2,1)} %bitcast.142) | data formatting | bytes 8388608 | tf_op jit(solution)/shard_map/reshape;reshape;squeeze | solution.py:37
  25.2 0.8 compare_convert_fusion.2
  26.6 6.2 fusion.15
  33.0 10.0 %while.60 = (s32[]{:T(128)}, f32[8,128,128]{2,1,0:T(8,128)S(1)}, f32[4,8,128,128]{3,2,1,0:T(8,128)S(1)}, f32[4,8,128,128]{3,2,1,0:T(8,128)}, f32[4]{0:T(128)S(1)}, /*index=5*/s32[]{:T(128)}, s32[]{:T(128)}) while((s32[]{:T(128)}, f32[8,128,128]{2,1,0:T(8,128)S(1)}, f32[4,8,128,128]{3,2,1,0:T(8,128)S(1)}, ...), condition=%wide.region_3.4_spmd.clone, body=%wide.region_2.3_spmd.clone.sunk | while | flops 524291 | bytes 2621560 | solution.py:84
  33.7 1.9 bitcast_add_fusion.13
  36.2 1.9 bitcast_add_fusion.13
  38.7 1.9 bitcast_add_fusion.13
  41.2 1.9 bitcast_add_fusion.13
  43.1 0.8 copy-done.1
  48.1 11.7 %all-reduce = f32[4]{0:T(128)S(1)} all-reduce(f32[4]{0:T(128)S(1)} %dynamic-update-slice), channel_id=1, replica_groups=mesh['seq'=4,'head'=4,'rep'=2] {'seq'}, use_global_device_ids=true, to_apply=%add | all-reduce | flops 4 | bytes 32
  59.8 5.3 copy.226
  65.1 7.6 %copy.184 = bf16[4,512,8,128]{1,3,2,0:T(8,128)(2,1)} copy(bf16[4,512,8,128]{3,2,1,0:T(8,128)(2,1)} %bitcast.144) | data formatting | bytes 8388608 | tf_op jit(solution)/shard_map/reshape;reshape;squeeze | solution.py:36
  72.8 2.4 and_convert_fusion
  75.2 11.6 %multiply_convert_fusion = bf16[4,8,512,512]{3,2,1,0:T(8,128)(2,1)} fusion(f32[4,512,512]{2,1,0:T(8,128)} %and_convert_fusion, bf16[4,512,8,128]{1,3,2,0:T(8,128)(2,1)} %copy.184, bf16[4,512,8,128]{1,3,2,0:T(8,128)(2,1)} %copy.175), kind=kOutput, calls=%fused_computation.8 | convolution fusion | flops 2164260864 | bytes 29360128 | tf_op jit(solution)/shard_map/nthe,nshe->nhts/dot_general | solution.py:48
  86.8 17.2 %fusion.24 = f32[4,8,512,128]{3,2,1,0:T(8,128)} fusion(bf16[4,8,512,512]{3,2,1,0:T(8,128)(2,1)} %multiply_convert_fusion, bf16[4,512,8,128]{3,2,1,0:T(8,128)(2,1)} %bitcast.138), kind=kOutput, calls=%fused_computation.39 | convolution fusion | flops 2147483648 | bytes 29360128 | tf_op jit(solution)/shard_map/nhts,nshe->nthe/dot_general | solution.py:56
  104.0 8.4 %bitcast_add_fusion.5 = f32[4,512,8,128]{3,1,2,0:T(8,128)S(1)} fusion(f32[4,8,512,128]{3,2,1,0:T(8,128)} %fusion.24, f32[4,512]{1,0:T(4,128)S(1)} %convert_element_type.133, f32[4,8,128,128]{3,2,1,0:T(8,128)S(1)} %copy-done.4, bf16[4,512,8,128]{1,3,2,0:T(8,128)(2,1)} %copy.184), kind=kOutput, calls=%fused_computation.16 | convolution fusion | flops 3225419776 | bytes 23076864 | tf_op jit(solution)/shard_map/nthe,nhef->nthf/dot_general | solution.py:88
  112.4 8.1 %copy.206 = f32[4,512,8,128]{3,2,1,0:T(8,128)} copy(f32[4,512,8,128]{3,1,2,0:T(8,128)S(1)} %bitcast_add_fusion.5) | data formatting | bytes 16777216 | tf_op jit(solution)/shard_map/add | solution.py:88
  120.5 9.4 %copy.209 = f32[2048,8,128]{0,2,1:T(8,128)} copy(f32[2048,8,128]{2,1,0:T(8,128)} %bitcast.146) | data formatting | bytes 16777216 | tf_op jit(solution)/shard_map/reshape | solution.py:102
  129.8 2.0 compare_convert_fusion
  131.8 11.0 %while.61 = (s32[]{:T(128)}, f32[8,128,128]{2,1,0:T(8,128)S(1)}, s32[]{:T(128)}, f32[4,8,128,128]{3,2,1,0:T(8,128)}, f32[4]{0:T(128)S(1)}, /*index=5*/s32[]{:T(128)}, f32[1]{0:T(128)}, s32[]{:T(128)}) while((s32[]{:T(128)}, f32[8,128,128]{2,1,0:T(8,128)S(1)}, s32[]{:T(128)}, f32[4,8,128,128]{3,2,1,0:T(8,128)}, f32[4]{0:T(128)S(1)}, ...), condition=%wide.region_5.6_spmd.clone, body=%wide.region_4.5_spmd.clone.sunk | while | flops 524293 | bytes 1573009 | solution.py:26
  133.1 1.5 fusion.60
  135.8 1.5 fusion.60
  138.6 1.5 fusion.60
  141.3 1.5 fusion.60
  142.8 10.8 %fusion.6 = bf16[2048,8,128]{0,2,1:T(8,128)(2,1)} fusion(f32[2048,8,128]{0,2,1:T(8,128)} %copy.209, f32[8,128,128]{2,1,0:T(8,128)S(1)} %get-tuple-element.364, bf16[2048,8,128]{2,1,0:T(8,128)(2,1)} %bitcast.145, f32[2048]{0:T(1024)S(1)} %get-tuple-element.507), kind=kOutput, calls=%fused_computation.15 | convolution fusion | flops 3227516928 | bytes 17309696 | tf_op jit(solution)/shard_map/the,hef->thf/dot_general | solution.py:138
  153.6 216.7 %all-gather.6.cloned.1.call-done = bf16[1,2048,4096]{2,1,0:T(8,128)(2,1)} async-done(((bf16[1,2048,1024]{2,1,0:T(8,128)(2,1)}), bf16[1,2048,4096]{2,1,0:T(8,128)(2,1)}) %all-gather.6.cloned.1.call-update) | async-done | bytes 16777232 | tf_op jit(solution)/shard_map/all_gather | solution.py:121
  370.3 24.1 %fusion.17 = bf16[2048,1024]{0,1:T(8,128)(2,1)} fusion(bf16[1024,4096]{1,0:T(8,128)(2,1)} %param.18, bf16[1,2048,4096]{2,1,0:T(8,128)(2,1)} %all-gather.6.cloned.1.call-done), kind=kOutput, calls=%fused_computation.34 | convolution fusion | flops 17181966336 | bytes 29360128 | tf_op jit(solution)/shard_map/dot_general | solution.py:122
  394.4 7.8 %reshape_reshape.3 = bf16[4,512,8,128]{1,0,3,2:T(4,128)(2,1)} reshape(bf16[2048,1024]{0,1:T(8,128)(2,1)} %fusion.17) | data formatting | bytes 8388608 | tf_op jit(solution)/shard_map/reshape;reshape | solution.py:39
  402.2 11.6 %multiply_convert_fusion.1 = bf16[4,8,512,512]{3,2,1,0:T(8,128)(2,1)} fusion(f32[4,512,512]{2,1,0:T(8,128)} %and_convert_fusion, bf16[4,512,8,128]{1,0,3,2:T(4,128)(2,1)} %reshape_reshape.3, bf16[4,512,8,128]{3,2,1,0:T(8,128)(2,1)} %bitcast.139), kind=kOutput, calls=%fused_computation.9 | convolution fusion | flops 2164260864 | bytes 29360128 | tf_op jit(solution)/shard_map/nthe,nshe->nhts/dot_general | solution.py:52
  413.9 14.7 %fusion.34 = f32[4,8,512,128]{3,2,1,0:T(8,128)} fusion(bf16[4,8,512,512]{3,2,1,0:T(8,128)(2,1)} %multiply_convert_fusion.1, bf16[4,512,8,128]{1,3,2,0:T(8,128)(2,1)} %copy.175), kind=kOutput, calls=%fused_computation.62 | convolution fusion | flops 2147483648 | bytes 29360128 | tf_op jit(solution)/shard_map/nhts,nshe->nthe/dot_general | solution.py:59
  428.6 6.5 fusion.13
  435.3 10.6 %while.62 = (s32[]{:T(128)}, f32[8,128,128]{2,1,0:T(8,128)S(1)}, f32[4,8,128,128]{3,2,1,0:T(8,128)S(1)}, f32[4,8,128,128]{3,2,1,0:T(8,128)}, f32[4]{0:T(128)S(1)}, /*index=5*/s32[]{:T(128)}, s32[]{:T(128)}, s32[]{:T(128)}) while((s32[]{:T(128)}, f32[8,128,128]{2,1,0:T(8,128)S(1)}, f32[4,8,128,128]{3,2,1,0:T(8,128)S(1)}, ...), condition=%wide.region_7.8_spmd.clone, body=%wide.region_6.7_spmd.clone.sunk | while | flops 524292 | bytes 2621580 | solution.py:85
  436.1 1.9 bitcast_add_fusion.14
  438.7 1.9 bitcast_add_fusion.14
  441.4 1.9 bitcast_add_fusion.14
  444.0 1.9 bitcast_add_fusion.14
  445.9 0.8 copy-done
  446.8 23.6 %fusion.2 = f32[1024,4096]{1,0:T(8,128)} fusion(bf16[2048,1024]{0,1:T(8,128)(2,1)} %bitcast.157, bf16[1,2048,4096]{2,1,0:T(8,128)(2,1)} %all-gather.6.cloned.1.call-done), kind=kOutput, calls=%fused_computation.10 | convolution fusion | flops 17179869184 | bytes 37748736 | tf_op jit(solution)/shard_map/dot_general | solution.py:155
  470.4 9.9 %bitcast_add_fusion.10 = f32[4,512,8,128]{3,1,2,0:T(8,128)S(1)} fusion(f32[4,8,512,128]{3,2,1,0:T(8,128)} %fusion.34, f32[4,512]{1,0:T(4,128)S(1)} %convert_element_type.133, f32[4,8,128,128]{3,2,1,0:T(8,128)} %copy-done.3, bf16[4,512,8,128]{1,0,3,2:T(4,128)(2,1)} %reshape_reshape.3), kind=kOutput, calls=%fused_computation.24 | convolution fusion | flops 3225419776 | bytes 23076864 | tf_op jit(solution)/shard_map/nthf,nhef->nthe/dot_general | solution.py:91
  480.3 8.1 %copy.179 = f32[4,512,8,128]{3,2,1,0:T(8,128)} copy(f32[4,512,8,128]{3,1,2,0:T(8,128)S(1)} %bitcast_add_fusion.10) | data formatting | bytes 16777216 | tf_op jit(solution)/shard_map/add | solution.py:91
  488.4 9.9 %copy.181 = f32[2048,8,128]{0,2,1:T(8,128)} copy(f32[2048,8,128]{2,1,0:T(8,128)} %bitcast.147) | data formatting | bytes 16777216 | tf_op jit(solution)/shard_map/reshape | solution.py:103
  498.2 10.8 %fusion.9 = bf16[2048,8,128]{0,2,1:T(8,128)(2,1)} fusion(f32[2048,8,128]{0,2,1:T(8,128)} %copy.181, f32[8,128,128]{2,1,0:T(8,128)S(1)} %get-tuple-element.364, bf16[2048,8,128]{0,2,1:T(8,128)(2,1)} %bitcast.150, f32[2048]{0:T(1024)S(1)} %get-tuple-element.507), kind=kOutput, calls=%fused_computation.23 | convolution fusion | flops 3227516928 | bytes 17309696 | tf_op jit(solution)/shard_map/thf,hef->the/dot_general | solution.py:141
  509.0 6.4 copy.210
  515.5 11.9 %fusion.35 = f32[4,8,512,128]{3,2,1,0:T(8,128)} fusion(bf16[4,8,512,512]{3,2,1,0:T(8,128)(2,1)} %multiply_convert_fusion.1, bf16[4,512,8,128]{1,3,2,0:T(8,128)(2,1)} %copy.184), kind=kOutput, calls=%fused_computation.63 | convolution fusion | flops 2147483648 | bytes 29360128 | tf_op jit(solution)/shard_map/nhts,nthe->nshe/dot_general | solution.py:60
  527.3 8.2 %bitcast_add_fusion.8 = f32[4,512,8,128]{3,1,2,0:T(8,128)S(1)} fusion(f32[4,8,512,128]{3,2,1,0:T(8,128)} %fusion.35, f32[4,512]{1,0:T(4,128)S(1)} %copy-done.6, f32[4,8,128,128]{3,2,1,0:T(8,128)S(1)} %get-tuple-element.365, bf16[4,512,8,128]{3,2,1,0:T(8,128)(2,1)} %bitcast.140), kind=kOutput, calls=%fused_computation.21 | convolution fusion | flops 3225419776 | bytes 23076864 | tf_op jit(solution)/shard_map/nshf,nhef->nshe/dot_general | solution.py:94
  535.5 8.1 %copy.188 = f32[4,512,8,128]{3,2,1,0:T(8,128)} copy(f32[4,512,8,128]{3,1,2,0:T(8,128)S(1)} %bitcast_add_fusion.8) | data formatting | bytes 16777216 | tf_op jit(solution)/shard_map/add | solution.py:94
  543.6 9.4 %copy.190 = f32[2048,8,128]{0,2,1:T(8,128)} copy(f32[2048,8,128]{2,1,0:T(8,128)} %bitcast.148) | data formatting | bytes 16777216 | tf_op jit(solution)/shard_map/reshape | solution.py:104
  553.1 7.7 %fusion.36 = f32[4,8,128,512]{2,3,1,0:T(8,128)} fusion(f32[4,8,128,128]{3,2,1,0:T(8,128)S(1)} %get-tuple-element.365, bf16[4,512,8,128]{1,3,2,0:T(8,128)(2,1)} %copy.175), kind=kOutput, calls=%fused_computation.64 | convolution fusion | flops 3221225472 | bytes 14680064 | tf_op jit(solution)/shard_map/nshe,nhef->nshf/dot_general | solution.py:97
  560.7 17.0 %add_bitcast_fusion = f32[4,512,8,128]{3,1,2,0:T(8,128)} fusion(f32[4,8,128,512]{2,3,1,0:T(8,128)} %fusion.36, f32[4,512]{1,0:T(4,128)S(1)} %copy-done.6, bf16[4,8,512,512]{3,2,1,0:T(8,128)(2,1)} %multiply_convert_fusion, bf16[4,512,8,128]{1,0,3,2:T(4,128)(2,1)} %reshape_reshape.3), kind=kOutput, calls=%fused_computation.25 | convolution fusion | flops 2151677952 | bytes 37756928 | tf_op jit(solution)/shard_map/nhts,nthe->nshe/dot_general | solution.py:63
  577.7 11.7 %copy.198 = f32[4,512,8,128]{3,2,1,0:T(8,128)} copy(f32[4,512,8,128]{3,1,2,0:T(8,128)} %add_bitcast_fusion) | data formatting | bytes 16777216 | tf_op jit(solution)/shard_map/add | solution.py:97
  589.4 9.4 %copy.201 = f32[2048,8,128]{0,2,1:T(8,128)} copy(f32[2048,8,128]{2,1,0:T(8,128)} %bitcast.149) | data formatting | bytes 16777216 | tf_op jit(solution)/shard_map/reshape | solution.py:105
  598.9 11.1 %while.63 = (s32[]{:T(128)}, f32[8,128,128]{2,1,0:T(8,128)S(1)}, s32[]{:T(128)}, f32[4,8,128,128]{3,2,1,0:T(8,128)}, f32[4]{0:T(128)S(1)}, /*index=5*/s32[]{:T(128)}, s32[]{:T(128)}, s32[]{:T(128)}, s32[]{:T(128)}, f32[1]{0:T(128)}) while((s32[]{:T(128)}, f32[8,128,128]{2,1,0:T(8,128)S(1)}, s32[]{:T(128)}, ...), condition=%wide.region_9.10_spmd.clone, body=%wide.region_8.9_spmd.clone.sunk | while | flops 524297 | bytes 1573071 | solution.py:26
  600.2 1.5 fusion.61
  603.0 1.5 fusion.61
  605.7 1.5 fusion.61
  608.5 1.5 fusion.61
  610.0 10.9 %fusion.8 = bf16[2048,8,128]{0,2,1:T(8,128)(2,1)} fusion(f32[2048,8,128]{0,2,1:T(8,128)} %copy.190, f32[8,128,128]{2,1,0:T(8,128)S(1)} %get-tuple-element.367, bf16[2048,8,128]{2,1,0:T(8,128)(2,1)} %bitcast.141, f32[2048]{0:T(1024)S(1)} %copy-done.7), kind=kOutput, calls=%fused_computation.20 | convolution fusion | flops 3227516928 | bytes 17309696 | tf_op jit(solution)/shard_map/thf,hef->the/dot_general | solution.py:144
  620.9 6.6 copy.211
  627.5 11.7 %fusion.7 = bf16[2048,8,128]{0,2,1:T(8,128)(2,1)} fusion(f32[2048,8,128]{0,2,1:T(8,128)} %copy.201, f32[8,128,128]{2,1,0:T(8,128)S(1)} %get-tuple-element.367, bf16[2048,8,128]{2,1,0:T(8,128)(2,1)} %bitcast.143, f32[2048]{0:T(1024)S(1)} %copy-done.7), kind=kOutput, calls=%fused_computation.18 | convolution fusion | flops 3227516928 | bytes 17309696 | tf_op jit(solution)/shard_map/the,hef->thf/dot_general | solution.py:147
  639.2 6.4 copy.212
  645.6 56.1 %all-reduce.3.cloned.1.call-done = f32[1024,4096]{1,0:T(8,128)} async-done(((f32[1024,4096]{1,0:T(8,128)}), f32[1024,4096]{1,0:T(8,128)}) %all-reduce.3.cloned.1.call-update) | async-done | bytes 16777232 | tf_op jit(solution)/shard_map/psum | solution.py:158
  701.7 3.1 constant_dynamic-slice_fusion
  (76 shorter events, 16.1 us)
Async XLA Ops:
  7.2 124.7 %all-gather.8.cloned.1.call-start = ((), (), s32[]{:S(2)}) async-start(), calls=%async_computation.2 | async-start | bytes 2621440 | tf_op jit(solution)/shard_map/all_gather | solution.py:13
  8.4 5.4 copy-start.5
  16.9 7.6 %copy-start.8 = (s32[1,7]{1,0:T(1,128)S(1)}, s32[1,7]{1,0:T(1,128)}, u32[]{:S(2)}) copy-start(s32[1,7]{1,0:T(1,128)} %param.19) | copy-start | bytes 88
  43.1 0.8 copy-start.1
  43.1 16.7 %copy-start.3 = (f32[4,8,128,128]{3,2,1,0:T(8,128)}, f32[4,8,128,128]{3,2,1,0:T(8,128)S(1)}, u32[]{:S(2)}) copy-start(f32[4,8,128,128]{3,2,1,0:T(8,128)S(1)} %get-tuple-element.362) | copy-start | bytes 6291460
  43.1 3.7 copy-start.11
  43.9 326.4 %all-gather.6.cloned.1.call-start = ((), (), s32[]{:S(2)}) async-start(), calls=%async_computation | async-start | bytes 20971520 | tf_op jit(solution)/shard_map/all_gather | solution.py:121
  44.6 554.2 %all-gather.10.cloned.1.call-start = ((), (), s32[]{:S(2)}) async-start(), calls=%async_computation.3 | async-start | bytes 2621440 | tf_op jit(solution)/shard_map/all_gather | solution.py:13
  86.8 17.2 %copy-start.4 = (f32[4,8,128,128]{3,2,1,0:T(8,128)S(1)}, f32[4,8,128,128]{3,2,1,0:T(8,128)}, u32[]{:S(2)}) copy-start(f32[4,8,128,128]{3,2,1,0:T(8,128)} %copy-done.3) | copy-start | bytes 6291460
  142.8 10.8 %copy-start.9 = (f32[4]{0:T(128)}, f32[4]{0:T(128)S(1)}, u32[]{:S(2)}) copy-start(f32[4]{0:T(128)S(1)} %get-tuple-element.750) | copy-start | bytes 52
  445.9 0.8 copy-start
  446.7 255.0 %all-reduce.3.cloned.1.call-start = ((), (), s32[]{:S(2)}) async-start(), calls=%async_computation.1 | async-start | bytes 33554432 | tf_op jit(solution)/shard_map/psum | solution.py:158
  515.5 11.9 %copy-start.6 = (f32[4,512]{1,0:T(4,128)S(1)}, f32[4,512]{1,0:T(4,128)}, u32[]{:S(2)}) copy-start(f32[4,512]{1,0:T(4,128)} %get-tuple-element.502) | copy-start | bytes 24580
  589.4 9.5 %copy-start.2 = (f32[8,128,128]{2,1,0:T(8,128)S(1)}, f32[8,128,128]{2,1,0:T(8,128)}, u32[]{:S(2)}) copy-start(f32[8,128,128]{2,1,0:T(8,128)} %custom-call.3) | copy-start | bytes 1572868
  589.4 9.5 %copy-start.10 = (f32[4]{0:T(128)S(1)}, f32[4]{0:T(128)}, u32[]{:S(2)}) copy-start(f32[4]{0:T(128)} %copy-done.9) | copy-start | bytes 52
  598.9 11.1 %copy-start.7 = (f32[2048]{0:T(1024)S(1)}, f32[2048]{0:T(1024)}, u32[]{:S(2)}) copy-start(f32[2048]{0:T(1024)} %get-tuple-element.506) | copy-start | bytes 24580
Sparse Core Ops, SparseCore 0:
  44.0 37.8 all-gather.7
  83.5 286.7 all-gather.5
  446.8 33.3 all-gather.9
  483.9 217.7 all-reduce.2
where the time goes:
time: 718 us; the launch traced here: 712 us
  waiting for transfers between devices  273 us (38%)
  matrix products  223 us (31%)
  local copies, waits for them, and re-layouts  147 us (20%)
  other arithmetic  34.7 us (5%)
  between operations  15.6 us (2%)
  blocking collectives  11.7 us (2%)
    all_gather x1, waiting for transfers between devices, on_device(): lax.all_gather(out_cotangent, 'head', axis=2, tiled=True)[0]  217 us
    psum x1, waiting for transfers between devices, on_device(): summed = lax.psum(partial_grad, ('seq', 'rep'))  56.1 us
    unnamed x33, local copies, waits for them, and re-layouts  36.1 us
    dot_general x1, matrix products, on_device(): lax.dot_general(full_cotangent, out_weight, (((1,), (1,)), ((), ())), pre...  24.1 us
    dot_general x1, matrix products, on_device(): lax.dot_general(attention_out, full_cotangent, (((0,), (0,)), ((), ())),...  23.6 us
    dot_general x1, matrix products, local_pass(): jnp.einsum('nhts,nshe->nthe', attn, value_blocks, preferred_element_type=...  17.2 us
    dot_general x1, matrix products, local_pass(): jnp.einsum('nhts,nthe->nshe', attn, grad_blocks, preferred_element_type=j...  17 us
    add x8, other arithmetic, link_step(): return (item[0] + item[1] * state, state)  15 us
  transfers between devices with their start and end apart: 4, of which 2 were waited for; matrix products, arithmetic and copies ran while one was open for 41% of the time, Pallas kernels for 0%

commit v1 on v0

--- a/solution.py
+++ b/solution.py
@@ -1,3 +1,4 @@
+import functools
 import jax
 import jax.numpy as jnp
 from jax import lax
@@ -6,6 +7,13 @@
 HD = 128
 BLOCK = 512
 highest = lax.Precision.HIGHEST
+
+
+def edit_indices(row_data, chip_axis):
+    return lax.all_gather(row_data, chip_axis).sum(axis=0)
+
+
+patches_post = functools.partial(edit_indices, chip_axis=("seq", "rep"))
 
 
 def prefix(shard, axis, combine, identity, reverse):
@@ -155,7 +163,7 @@
     partial_grad = lax.dot_general(
         attention_out, full_cotangent, (((0,), (0,)), ((), ())), preferred_element_type=jnp.float32
     )
-    summed = lax.psum(partial_grad, ("seq", "rep"))
+    summed = patches_post(partial_grad)
     columns = summed.shape[1] // lax.axis_size(("seq", "rep"))
     grad_weight = lax.dynamic_slice_in_dim(
         summed, lax.axis_index(("seq", "rep")) * columns, columns, 1

time: 718 us -> 1100 us (1.53)
  waiting for transfers between devices: 273 us -> 611 us
  other arithmetic: 34.7 us -> 82 us
    all_gather x0 -> x1, waiting for transfers between devices: none -> 393 us  [edit_indices(): return lax.all_gather(row_data, chip_axis).sum(axis=0)]
    psum x1 -> x0, waiting for transfers between devices: 56.1 us -> none  [on_device(): summed = lax.psum(partial_grad, ('seq', 'rep'))]
    reduce_sum x0 -> x1, other arithmetic: none -> 47.2 us  [edit_indices(): return lax.all_gather(row_data, chip_axis).sum(axis=0)]
    unnamed x33 -> x31, local copies, waits for them, and re-layouts: 36.1 us -> 36.4 us
  transfers between devices with their start and end apart: 4 -> 4, of which waited for: 2 -> 2; matrix products, arithmetic and copies ran while one was open for 41% -> 29% of each run, Pallas kernels for 0% -> 0%
where the time goes in v1:
time: 1100 us
  waiting for transfers between devices  611 us (56%)
  matrix products  221 us (20%)
  local copies, waits for them, and re-layouts  150 us (14%)
  other arithmetic  82 us (7%)
  between operations  15.6 us (1%)
  blocking collectives  11.6 us (1%)
    all_gather x1, waiting for transfers between devices, edit_indices(): return lax.all_gather(row_data, chip_axis).sum(axis=0)  393 us
    all_gather x1, waiting for transfers between devices, on_device(): lax.all_gather(out_cotangent, 'head', axis=2, tiled=True)[0]  217 us
    reduce_sum x1, other arithmetic, edit_indices(): return lax.all_gather(row_data, chip_axis).sum(axis=0)  47.2 us
    unnamed x31, local copies, waits for them, and re-layouts  36.4 us
    dot_general x1, matrix products, on_device(): lax.dot_general(full_cotangent, out_weight, (((1,), (1,)), ((), ())), pre...  24.1 us
    dot_general x1, matrix products, on_device(): lax.dot_general(attention_out, full_cotangent, (((0,), (0,)), ((), ())),...  23.7 us
  transfers between devices with their start and end apart: 4, of which 2 were waited for; matrix products, arithmetic and copies ran while one was open for 29% of the time, Pallas kernels for 0%

profile of v1, /device:TPU:0, one launch (start us, length us, event | category | flops | bytes accessed | tf_op | source)
XLA Modules:
  0.0 1096.4 jit_solution(1913916512082089097)
XLA Ops:
  8.4 1.3 fusion.31
  11.0 5.3 copy.225
  16.3 7.5 copy.175
  23.8 3.5 copy.224
  27.3 2.7 fusion.15
  30.3 10.0 while.60
  30.9 1.9 bitcast_add_fusion.13
  33.4 1.9 bitcast_add_fusion.13
  35.9 1.9 bitcast_add_fusion.13
  38.5 1.9 bitcast_add_fusion.13
  45.2 11.6 %all-reduce = f32[4]{0:T(128)S(1)} all-reduce(f32[4]{0:T(128)S(1)} %dynamic-update-slice), channel_id=1, replica_groups=mesh['seq'=4,'head'=4,'rep'=2] {'seq'}, use_global_device_ids=true, to_apply=%add | all-reduce | flops 4 | bytes 32
  56.9 5.3 copy.226
  62.2 7.5 copy.184
  69.8 2.4 and_convert_fusion
  72.2 11.6 %multiply_convert_fusion = bf16[4,8,512,512]{3,2,1,0:T(8,128)(2,1)} fusion(f32[4,512,512]{2,1,0:T(8,128)} %and_convert_fusion, bf16[4,512,8,128]{1,3,2,0:T(8,128)(2,1)} %copy.184, bf16[4,512,8,128]{1,3,2,0:T(8,128)(2,1)} %copy.175), kind=kOutput, calls=%fused_computation.8 | convolution fusion | flops 2164260864 | bytes 29360128 | tf_op jit(solution)/shard_map/nthe,nshe->nhts/dot_general | solution.py:56
  83.8 17.2 %fusion.24 = f32[4,8,512,128]{3,2,1,0:T(8,128)} fusion(bf16[4,8,512,512]{3,2,1,0:T(8,128)(2,1)} %multiply_convert_fusion, bf16[4,512,8,128]{3,2,1,0:T(8,128)(2,1)} %bitcast.139), kind=kOutput, calls=%fused_computation.39 | convolution fusion | flops 2147483648 | bytes 29360128 | tf_op jit(solution)/shard_map/nhts,nshe->nthe/dot_general | solution.py:64
  101.0 8.4 bitcast_add_fusion.5
  109.4 8.1 copy.206
  117.5 9.4 copy.209
  126.9 1.9 compare_convert_fusion
  128.8 10.9 while.61
  130.0 1.5 fusion.60
  132.7 1.5 fusion.60
  135.5 1.5 fusion.60
  138.2 1.5 fusion.60
  139.7 10.8 fusion.6
  150.5 217.0 %all-gather.8.cloned.1.call-done = bf16[1,2048,4096]{2,1,0:T(8,128)(2,1)} async-done(((bf16[1,2048,1024]{2,1,0:T(8,128)(2,1)}), bf16[1,2048,4096]{2,1,0:T(8,128)(2,1)}) %all-gather.8.cloned.1.call-update) | async-done | bytes 16777232 | tf_op jit(solution)/shard_map/all_gather | solution.py:129
  367.5 24.1 %fusion.17 = bf16[2048,1024]{0,1:T(8,128)(2,1)} fusion(bf16[1024,4096]{1,0:T(8,128)(2,1)} %param.18, bf16[1,2048,4096]{2,1,0:T(8,128)(2,1)} %all-gather.8.cloned.1.call-done), kind=kOutput, calls=%fused_computation.34 | convolution fusion | flops 17181966336 | bytes 29360128 | tf_op jit(solution)/shard_map/dot_general | solution.py:130
  391.7 7.9 reshape_reshape.3
  399.6 6.5 fusion.13
  406.3 10.0 while.62
  407.0 1.8 bitcast_add_fusion.14
  409.5 1.8 bitcast_add_fusion.14
  412.0 1.8 bitcast_add_fusion.14
  414.5 1.8 bitcast_add_fusion.14
  416.3 0.8 copy-done.2
  417.2 23.7 %fusion.2 = f32[1024,4096]{1,0:T(8,128)} fusion(bf16[2048,1024]{0,1:T(8,128)(2,1)} %bitcast.158, bf16[1,2048,4096]{2,1,0:T(8,128)(2,1)} %all-gather.8.cloned.1.call-done), kind=kOutput, calls=%fused_computation.10 | convolution fusion | flops 17179869184 | bytes 37748736 | tf_op jit(solution)/shard_map/dot_general | solution.py:163
  440.9 11.7 %multiply_convert_fusion.1 = bf16[4,8,512,512]{3,2,1,0:T(8,128)(2,1)} fusion(f32[4,512,512]{2,1,0:T(8,128)} %and_convert_fusion, bf16[4,512,8,128]{1,0,3,2:T(4,128)(2,1)} %reshape_reshape.3, bf16[4,512,8,128]{3,2,1,0:T(8,128)(2,1)} %bitcast.140), kind=kOutput, calls=%fused_computation.9 | convolution fusion | flops 2164260864 | bytes 29360128 | tf_op jit(solution)/shard_map/nthe,nshe->nhts/dot_general | solution.py:60
  452.6 13.4 %fusion.35 = f32[4,8,512,128]{3,2,1,0:T(8,128)} fusion(bf16[4,8,512,512]{3,2,1,0:T(8,128)(2,1)} %multiply_convert_fusion.1, bf16[4,512,8,128]{1,3,2,0:T(8,128)(2,1)} %copy.184), kind=kOutput, calls=%fused_computation.63 | convolution fusion | flops 2147483648 | bytes 29360128 | tf_op jit(solution)/shard_map/nhts,nthe->nshe/dot_general | solution.py:68
  466.0 11.9 %bitcast_add_fusion.8 = f32[4,512,8,128]{3,1,2,0:T(8,128)S(1)} fusion(f32[4,8,512,128]{3,2,1,0:T(8,128)} %fusion.35, f32[4,512]{1,0:T(4,128)S(1)} %copy-done.6, f32[4,8,128,128]{3,2,1,0:T(8,128)S(1)} %get-tuple-element.365, bf16[4,512,8,128]{3,2,1,0:T(8,128)(2,1)} %bitcast.141), kind=kOutput, calls=%fused_computation.21 | convolution fusion | flops 3225419776 | bytes 23076864 | tf_op jit(solution)/shard_map/nshf,nhef->nshe/dot_general | solution.py:102
  477.9 10.4 copy.188
  488.3 9.9 copy.190
  498.2 14.7 %fusion.34 = f32[4,8,512,128]{3,2,1,0:T(8,128)} fusion(bf16[4,8,512,512]{3,2,1,0:T(8,128)(2,1)} %multiply_convert_fusion.1, bf16[4,512,8,128]{1,3,2,0:T(8,128)(2,1)} %copy.175), kind=kOutput, calls=%fused_computation.62 | convolution fusion | flops 2147483648 | bytes 29360128 | tf_op jit(solution)/shard_map/nhts,nshe->nthe/dot_general | solution.py:67
  512.9 10.2 bitcast_add_fusion.10
  523.2 8.1 copy.179
  531.2 9.5 copy.181
  540.8 10.5 fusion.9
  551.3 6.4 copy.210
  557.7 7.7 fusion.36
  565.3 14.8 %add_bitcast_fusion = f32[4,512,8,128]{3,1,2,0:T(8,128)} fusion(f32[4,8,128,512]{2,3,1,0:T(8,128)} %fusion.36, f32[4,512]{1,0:T(4,128)S(1)} %copy-done.6, bf16[4,8,512,512]{3,2,1,0:T(8,128)(2,1)} %multiply_convert_fusion, bf16[4,512,8,128]{1,0,3,2:T(4,128)(2,1)} %reshape_reshape.3), kind=kOutput, calls=%fused_computation.25 | convolution fusion | flops 2151677952 | bytes 37756928 | tf_op jit(solution)/shard_map/nhts,nthe->nshe/dot_general | solution.py:71
  580.1 11.5 %copy.198 = f32[4,512,8,128]{3,2,1,0:T(8,128)} copy(f32[4,512,8,128]{3,1,2,0:T(8,128)} %add_bitcast_fusion) | data formatting | bytes 16777216 | tf_op jit(solution)/shard_map/add | solution.py:105
  591.6 9.4 copy.201
  601.0 11.0 %while.63 = (s32[]{:T(128)}, f32[8,128,128]{2,1,0:T(8,128)S(1)}, s32[]{:T(128)}, f32[4,8,128,128]{3,2,1,0:T(8,128)}, f32[4]{0:T(128)S(1)}, /*index=5*/s32[]{:T(128)}, s32[]{:T(128)}, s32[]{:T(128)}, s32[]{:T(128)}, f32[1]{0:T(128)}) while((s32[]{:T(128)}, f32[8,128,128]{2,1,0:T(8,128)S(1)}, s32[]{:T(128)}, ...), condition=%wide.region_9.10_spmd.clone, body=%wide.region_8.9_spmd.clone.sunk | while | flops 524297 | bytes 1573071 | solution.py:34
  602.2 1.5 fusion.61
  605.0 1.5 fusion.61
  607.7 1.5 fusion.61
  610.5 1.5 fusion.61
  612.0 10.6 fusion.8
  622.5 6.6 copy.211
  629.1 10.7 fusion.7
  639.9 6.4 copy.212
  646.3 393.0 %all-gather.14.cloned.1.call-done = f32[8192,4096]{1,0:T(8,128)} async-done(((f32[1024,4096]{1,0:T(8,128)}), f32[8192,4096]{1,0:T(8,128)}) %all-gather.14.cloned.1.call-update) | async-done | bytes 134217744 | tf_op jit(solution)/shard_map/all_gather | solution.py:13
  1039.2 47.2 %reduce_sum.32 = f32[1024,4096]{1,0:T(8,128)} reduce(f32[8,1024,4096]{2,1,0:T(8,128)} %bitcast.28, f32[]{:T(128)} %constant.146.clone.1), dimensions={0}, to_apply=%region_10.11 | reduce | flops 29360128 | bytes 150994944 | tf_op jit(solution)/shard_map/reduce_sum | solution.py:13
  1086.5 3.1 constant_dynamic-slice_fusion
  (75 shorter events, 16.5 us)
Async XLA Ops:
  7.2 121.6 %all-gather.10.cloned.1.call-start = ((), (), s32[]{:S(2)}) async-start(), calls=%async_computation.1 | async-start | bytes 2621440 | tf_op jit(solution)/shard_map/all_gather | solution.py:21
  23.8 3.5 copy-start.1
  27.3 2.8 copy-start
  40.3 0.8 copy-start.3
  40.3 16.5 %copy-start.4 = (f32[4,8,128,128]{3,2,1,0:T(8,128)}, f32[4,8,128,128]{3,2,1,0:T(8,128)S(1)}, u32[]{:S(2)}) copy-start(f32[4,8,128,128]{3,2,1,0:T(8,128)S(1)} %get-tuple-element.362) | copy-start | bytes 6291460
  40.3 3.5 copy-start.10
  41.1 326.4 %all-gather.8.cloned.1.call-start = ((), (), s32[]{:S(2)}) async-start(), calls=%async_computation | async-start | bytes 20971520 | tf_op jit(solution)/shard_map/all_gather | solution.py:129
  41.9 559.1 %all-gather.12.cloned.1.call-start = ((), (), s32[]{:S(2)}) async-start(), calls=%async_computation.2 | async-start | bytes 2621440 | tf_op jit(solution)/shard_map/all_gather | solution.py:21
  83.8 17.2 %copy-start.5 = (f32[4,8,128,128]{3,2,1,0:T(8,128)S(1)}, f32[4,8,128,128]{3,2,1,0:T(8,128)}, u32[]{:S(2)}) copy-start(f32[4,8,128,128]{3,2,1,0:T(8,128)} %copy-done.4) | copy-start | bytes 6291460
  139.7 10.8 copy-start.8
  416.3 0.8 copy-start.2
  417.2 622.1 %all-gather.14.cloned.1.call-start = ((), (), s32[]{:S(2)}) async-start(), calls=%async_computation.3 | async-start | bytes 150994944 | tf_op jit(solution)/shard_map/all_gather | solution.py:13
  452.6 13.4 %copy-start.6 = (f32[4,512]{1,0:T(4,128)S(1)}, f32[4,512]{1,0:T(4,128)}, u32[]{:S(2)}) copy-start(f32[4,512]{1,0:T(4,128)} %get-tuple-element.502) | copy-start | bytes 24580
  591.6 9.4 copy-start.9
  600.9 11.0 %copy-start.7 = (f32[2048]{0:T(1024)S(1)}, f32[2048]{0:T(1024)}, u32[]{:S(2)}) copy-start(f32[2048]{0:T(1024)} %get-tuple-element.506) | copy-start | bytes 24580
Sparse Core Ops, SparseCore 0:
  41.3 37.8 all-gather.9
  80.8 286.7 all-gather.7
  417.3 33.3 all-gather.11
  452.4 586.7 all-gather.13
